TPU v7x, 32 devices: a whole 2x2x4 slice. The times are simulated.
32 devices in a mesh: groups: 2 (over x), tok: 16 (over z, y, core).
Axes of the slice: x: 2, y: 2, z: 4, core: 2. Of those that a mesh axis runs over, the one named last changes fastest.
Arguments:
- tokens: bfloat16 [8192, 1024], P(('groups', 'tok')), parts along dimension 0, may hold values from -6 to 6
- norm_gain: float32 [1024], replicated, may hold values from 0.1 to 1.9
- w_qk: bfloat16 [1024, 1024], replicated, may hold values from -0.1875 to 0.1875
- w_v: bfloat16 [1024, 1024], replicated, may hold values from -0.1875 to 0.1875
- cotangent: bfloat16 [8192, 1024], P(('groups', 'tok')), parts along dimension 0, may hold values from -48 to 48
- log_sums: float32 [2, 8, 8192], P(None, None, ('groups', 'tok')), parts along dimension 2, may hold values from 7 to 8
- bucket_order: int32 [2, 8192], P(None, 'groups'), parts along dimension 1, may hold values from 0 to 4095, as said below
- token_position: int32 [2, 8192], P(None, ('groups', 'tok')), parts along dimension 1, may hold values from 0 to 4095, as said below
Outputs:
- d_tokens: bfloat16 [8192, 1024], P(('groups', 'tok')), parts along dimension 0
- d_gain: float32 [2048], P(('groups', 'tok')), parts along dimension 0
- d_wqk: float32 [2048, 1024], P(('groups', 'tok')), parts along dimension 0
- d_wv: float32 [2048, 1024], P(('groups', 'tok')), parts along dimension 0
There are 2 independent parts, one for each index of `groups`. A program takes and returns all parts, laid end to end along the dimension named above; an argument that names none is the same for every part. Nothing has to cross between parts.
Inputs may be any that keep to these rules, and one draw needn't show every extreme that they name: `bucket_order`: each row is a permutation; the 256 hash-sorted positions of one device hold at most 20 tokens of any one device's 256 tokens, and exactly 20 of at least one. token_position[r, bucket_order[r, p]] = p.
All inputs are finite; a program needn't handle non-finite values.
Results may differ from a plain program's by a relative error of at most 0.025.
Values may be sent and summed in bfloat16 or wider, within the bound.
A program may use at most 128 MiB of HBM per device.

v0:
```python
import functools
import math

import jax
import jax.numpy as jnp
from jax import lax
from jax.experimental import pallas as pl
from jax.experimental.pallas import tpu as pltpu
from jax.sharding import PartitionSpec as P

BLOCK = 256
EPS = 1e-06
VMEM_LIMIT = 63 * 1024 * 1024
MESH = pl.DeviceIdType.MESH
F32 = jnp.float32
BF16 = jnp.bfloat16


def whole(count):
    return [pl.BlockSpec(memory_space=pltpu.VMEM)] * count


def dot_nn(a, b):
    return lax.dot_general(a, b, (((1,), (0,)), ((), ())), preferred_element_type=F32)


def dot_nt(a, b):
    return lax.dot_general(a, b, (((1,), (1,)), ((), ())), preferred_element_type=F32)


def dot_tn(a, b):
    return lax.dot_general(a, b, (((0,), (0,)), ((), ())), preferred_element_type=F32)


def slot_row(order, tok_dev, stride):
    size = order.shape[1]
    owner = lax.div(order, jnp.int32(tok_dev))
    owner_col = jnp.broadcast_to(owner, (size, size)).T
    before = lax.broadcasted_iota(jnp.int32, (size, size), 0) < lax.broadcasted_iota(
        jnp.int32, (size, size), 1
    )
    earlier = (owner_col == owner) & before
    rank = jnp.sum(earlier.astype(F32), axis=0, keepdims=True).astype(jnp.int32)
    return owner * stride + rank


def one_hot_rows(slots, slot_count):
    size = slots.shape[1]
    ids = lax.broadcasted_iota(jnp.int32, (slot_count, size), 0)
    return jnp.where(ids == slots, 1.0, 0.0).astype(BF16)


def normal_of(x, gain):
    return (x * lax.rsqrt(jnp.mean(x * x, axis=-1, keepdims=True) + EPS) * gain).astype(BF16)


def unit_of(q):
    depth = q.shape[-1]
    scale = lax.rsqrt(jnp.mean(q * q, axis=-1, keepdims=True) + EPS)
    return (q * scale / math.sqrt(depth)).astype(BF16)


def flipped(index, mask):
    bit = 1
    while bit <= mask:
        if mask & bit:
            index = index + bit * (1 - 2 * lax.rem(lax.div(index, bit), 2))
        bit *= 2
    return index


def forwarding_order(masks):
    return sorted(masks, key=lambda m: int(bin(m)[:1:-1].ljust(16, "0"), 2), reverse=True)


def looped(count, unroll, body):
    steps = count // unroll

    def step(i, carry):
        for u in range(unroll):
            body(i * unroll + u)
        return carry

    if steps > 1:
        lax.fori_loop(0, steps, step, 0)
    for i in range(steps * unroll if steps > 1 else 0, count):
        body(i)


def core_kernel(heads, stride, split, grad_scale, *refs):
    gain_hbm, order_hbm, sums_hbm, tokens_hbm, cot_hbm, qk_hbm, v_hbm = refs[:7]
    d_tokens_ref, d_gain_ref, d_qk_ref, d_v_ref = refs[7:11]
    (
        gain_ref, order_ref, sums_ref, tokens_ref, cot_ref, qk_ref, v_ref,
        normal, slab_out, slab_in, sums_out, sums_in_rows, spread, pick, bucket,
        sorted_q, sorted_k, sorted_g, sorted_v, probs, key_own, key_before, d_query,
        part_out, part_in, home_out, home_in, grads,
        gain_out, gain_back, weights, sums_in, sums_run,
        load_sem, slab_sem, relay_sem, rows_sem, part_sem, home_sem, gain_sem, sums_sem,
    ) = refs[11:]
    devices = lax.axis_size("tok")
    me = lax.axis_index("tok")
    rounds, seq_len = order_ref.shape
    rows, width = tokens_ref.shape
    depth = width // heads
    chips = devices // rounds
    chip, lane = lax.div(me, rounds), lax.rem(me, rounds)
    blocks = seq_len // rows
    queries = blocks // split
    first = lax.rem(chip, split) * queries
    base = 1 if split == 1 else 0
    held = queries + 1 - base
    slot_count = devices * stride
    parts = [slice(head * depth, (head + 1) * depth) for head in range(heads)]

    def remote(src, dst, sems, peer):
        return pltpu.make_async_remote_copy(
            src_ref=src,
            dst_ref=dst,
            send_sem=sems.at[0],
            recv_sem=sems.at[1],
            device_id={"tok": peer},
            device_id_type=MESH,
        )

    barrier = pltpu.get_barrier_semaphore()
    for step in range(1, devices):
        peer = lax.rem(me + step, devices)
        pl.semaphore_signal(barrier, inc=1, device_id={"tok": peer}, device_id_type=MESH)
    loads = {
        name: pltpu.make_async_copy(src, dst, load_sem.at[place])
        for place, (name, src, dst) in enumerate(
            [
                ("tokens", tokens_hbm, tokens_ref),
                ("gain", gain_hbm, gain_ref),
                ("qk", qk_hbm, qk_ref),
                ("sums", sums_hbm, sums_ref),
                ("cot", cot_hbm, cot_ref),
                ("order", order_hbm, order_ref),
                ("v", v_hbm, v_ref),
            ]
        )
    }
    for load in loads.values():
        load.start()

    def chip_at(step):
        return lax.rem(chip + step, chips)

    def chip_behind(step):
        return lax.rem(chip + chips - step, chips)

    def lane_at(step):
        return lax.rem(lane + step, rounds)

    def lane_behind(step):
        return lax.rem(lane + rounds - step, rounds)

    slabs = [
        {
            step: remote(
                slab_out.at[t, lax.div(chip_at(step), split)],
                slab_in.at[t, lane, chip],
                slab_sem.at[t, step - 1],
                chip_at(step) * rounds + lane,
            )
            for step in range(1, chips)
        }
        for t in range(3)
    ]
    relays = [
        {
            (d, step): remote(
                slab_in.at[t, lane, chip_behind(step)],
                slab_in.at[t, lane, chip_behind(step)],
                relay_sem.at[t, d - 1, step],
                chip * rounds + lane_at(d),
            )
            for d in range(1, rounds)
            for step in range(chips)
        }
        for t in range(3)
    ]
    row_sums = []
    for step in range(1, devices):
        peer = lax.rem(me + step, devices)
        unit = lax.div(lax.div(peer, rounds), split) * rounds + lax.rem(peer, rounds)
        row_sums.append(remote(sums_out.at[unit], sums_in_rows.at[me], rows_sem.at[step - 1], peer))
    shares = [
        {
            (d, step): remote(
                part_out.at[d - 1, step],
                part_in.at[t, d - 1, step],
                part_sem.at[t, d - 1, step],
                chip * rounds + lane_at(d),
            )
            for d in range(1, rounds)
            for step in range(chips)
        }
        for t in range(2)
    ]
    homes = [
        {
            step: remote(
                home_out.at[t, step],
                home_in.at[t, chip],
                home_sem.at[t, step - 1],
                chip_at(step) * rounds + lane,
            )
            for step in range(1, chips)
        }
        for t in range(2)
    ]
    gains = []
    for step in range(1, devices):
        peer = lax.rem(me + step, devices)
        gains.append(remote(gain_out.at[peer], gain_back.at[me], gain_sem.at[step - 1], peer))

    bits = devices.bit_length() - 1
    first_slot = [devices - (devices >> k) for k in range(bits)]
    bit_orders = [list(range(bits)), [0, *range(2, bits), 1]]
    streams = len(bit_orders)
    piece = width // streams

    def physical(stream, mask):
        return sum(1 << bit_orders[stream][k] for k in range(bits) if mask >> k & 1)

    def sums_copy(half, stream, k, mask):
        slot = first_slot[k] + (mask >> (k + 1))
        if k == 0:
            source = weights.at[half, stream, flipped(me, physical(stream, mask))]
        else:
            source = sums_run.at[half, stream, mask >> 1]
        peer = flipped(me, 1 << bit_orders[stream][k])
        return remote(
            source, sums_in.at[half, stream, slot], sums_sem.at[half, stream, slot], peer
        )

    stages = [
        [
            [
                {m: sums_copy(half, stream, k, m) for m in range(1 << k, devices, 2 << k)}
                for stream in range(streams)
            ]
            for half in range(2)
        ]
        for k in range(bits)
    ]
    far_first = sorted(range(1, chips), key=lambda step: -min(step, chips - step))
    near_first = far_first[::-1]

    def send_slabs(t):
        for step in far_first:
            slabs[t][step].start()
        slab_in[t, lane, chip] = slab_out[t, lax.div(chip, split)]

    with jax.named_scope("first"):
        loads["tokens"].wait()
        loads["gain"].wait()
        normal[...] = normal_of(tokens_ref[...].astype(F32), gain_ref[...])
        loads["qk"].wait()
        query = dot_nn(normal[...], qk_ref[...]).astype(BF16)
        for head, part in enumerate(parts):
            slab_out[0, head] = query[:, part]
        loads["sums"].wait()
        for hashing in range(rounds):
            for head in range(heads):
                sums_out[head * rounds + hashing] = sums_ref[hashing, head : head + 1, :]
        loads["cot"].wait()
        for head, part in enumerate(parts):
            slab_out[1, head] = cot_ref[:, part]
    with jax.named_scope("barrier"):
        pl.semaphore_wait(barrier, devices - 1)
    with jax.named_scope("sends"):
        for copy in row_sums:
            copy.start()
        send_slabs(0)
        own_unit = lax.div(chip, split) * rounds + lane
        sums_in_rows[me] = sums_out[own_unit]
        send_slabs(1)
        loads["v"].wait()
        value = dot_nn(normal[...], v_ref[...]).astype(BF16)
        for head, part in enumerate(parts):
            slab_out[2, head] = value[:, part]
        send_slabs(2)
        for t in range(3):
            for d in range(1, rounds):
                relays[t][d, 0].start()
        loads["order"].wait()

    token_ids = lax.broadcasted_iota(jnp.int32, (rows, rows), 0)

    def tables(place):
        block = lax.rem(first + (place + base - 1 + blocks), blocks)
        start = pl.multiple_of(block * rows, rows)
        order = order_ref[pl.ds(lane, 1), pl.ds(start, rows)]
        chosen = one_hot_rows(slot_row(order, rows, stride), slot_count)
        pick[place] = chosen
        within = jnp.where(token_ids == lax.rem(order, jnp.int32(rows)), 1.0, 0.0).astype(BF16)
        moved = dot_nt(chosen, within).astype(BF16)
        spread[:, place] = moved.reshape(devices, stride, rows)

    with jax.named_scope("tables"):
        looped(held, 4, tables)

    def bucket_rows(t, source_chip, source_lane):
        source = source_chip * rounds + source_lane
        table = spread[source].reshape(held * stride, rows)
        placed = dot_nn(table, slab_in[t, source_lane, source_chip]).astype(BF16)
        bucket[source] = placed.reshape(held, stride, depth)

    def take_slabs(t):
        with jax.named_scope(f"take{t}"):
            for step in near_first:
                slabs[t][step].wait_recv()
                for d in range(1, rounds):
                    relays[t][d, step].start()

    def gather(t):
        with jax.named_scope(f"gather{t}"):
            looped(chips, 8, lambda step: bucket_rows(t, chip_behind(step), lane))
            for d in range(1, rounds):
                for step in [0, *near_first]:
                    relays[t][d, step].wait_recv()
                looped(chips, 8, lambda step: bucket_rows(t, chip_behind(step), lane_behind(d)))

    def sorted_rows(place):
        data = bucket[:, place].reshape(slot_count, depth)
        return dot_tn(pick[place], data).astype(BF16)

    def sort_queries(place):
        q = sorted_rows(place)
        sorted_q[place + base] = q
        sorted_k[place + base] = unit_of(q.astype(F32))

    take_slabs(0)
    gather(0)
    with jax.named_scope("sortq"):
        looped(held, 4, sort_queries)
    if split == 1:
        sorted_k[0] = sorted_k[queries]
    with jax.named_scope("rowsums"):
        for copy in row_sums:
            copy.wait_recv()
    diagonal = lax.broadcasted_iota(jnp.int32, (2 * rows, rows), 0) == rows + (
        lax.broadcasted_iota(jnp.int32, (2 * rows, rows), 1)
    )

    def probabilities(i):
        keys = sorted_k[pl.ds(i, 2)].reshape(2 * rows, depth)
        scores = dot_nt(keys, sorted_q[i + 1]) - sums_in_rows[first + i]
        probs[i + 1] = jnp.where(diagonal, 0.0, jnp.exp(scores)).astype(BF16)

    with jax.named_scope("probs"):
        looped(queries, 4, probabilities)
    if split > 1:
        probs[0] = jnp.zeros((2 * rows, rows), BF16)
        probs[queries + 1] = jnp.zeros((2 * rows, rows), BF16)
        sorted_g[queries + 1] = jnp.zeros((rows, depth), BF16)

    def after(j):
        return lax.rem(j, queries) + 1 if split == 1 else j + 1

    def bucket_back(place, grad):
        placed = dot_nn(pick[place], grad).astype(BF16)
        bucket[:, place] = placed.reshape(devices, stride, depth)

    def home_rows(source_chip, source_lane):
        source = source_chip * rounds + source_lane
        table = spread[source].reshape(held * stride, rows)
        return dot_tn(table, bucket[source].reshape(held * stride, depth))

    def send_home(t):
        with jax.named_scope(f"home{t}"):
            if t > 0:
                for copy in shares[t - 1].values():
                    copy.wait_send()
            for d in range(1, rounds):

                def share(step):
                    part_out[d - 1, step] = home_rows(chip_at(step), lane_at(d)).astype(BF16)

                looped(chips, 8, share)
                for step in [*far_first, 0]:
                    shares[t][d, step].start()

            def keep(step):
                d_query[step] = home_rows(chip_at(step), lane)

            looped(chips, 8, keep)
            for step in [*far_first, 0]:
                for d in range(1, rounds):
                    shares[t][d, step].wait_recv()

            for step in [*far_first, 0]:
                total = d_query[step]
                for d in range(1, rounds):
                    total += part_in[t, d - 1, step].astype(F32)
                home_out[t, step] = total.astype(BF16)
            for step in far_first:
                homes[t][step].start()
            home_in[t, chip] = home_out[t, 0]

    take_slabs(1)
    gather(1)

    def sort_cotangents(place):
        sorted_g[place + base] = sorted_rows(place)

    def value_gradients(place):
        j = place + base
        grad = dot_nn(probs[j, rows:, :], sorted_g[j])
        grad += dot_nn(probs[after(j), :rows, :], sorted_g[after(j)])
        bucket_back(place, grad.astype(BF16))

    with jax.named_scope("sortg"):
        looped(held, 16, sort_cotangents)
    with jax.named_scope("dv"):
        looped(held, 16, value_gradients)
    send_home(0)
    take_slabs(2)
    gather(2)

    def sort_values(place):
        sorted_v[place + base] = sorted_rows(place)

    with jax.named_scope("sortv"):
        looped(held, 16, sort_values)
    if split == 1:
        sorted_v[0] = sorted_v[queries]
    else:
        key_own[0] = jnp.zeros((rows, depth), F32)
        d_query[0] = jnp.zeros((rows, depth), F32)
        key_before[queries + 1] = jnp.zeros((rows, depth), F32)

    def score_gradients(i):
        j = i + 1
        values = sorted_v[pl.ds(i, 2)].reshape(2 * rows, depth)
        keys = sorted_k[pl.ds(i, 2)].reshape(2 * rows, depth)
        w = probs[j].astype(F32)
        d_probs = dot_nt(values, sorted_g[j])
        delta = jnp.sum(w * d_probs, axis=0, keepdims=True)
        d_scores = (w * (d_probs - delta)).astype(BF16)
        d_query[j] = dot_tn(d_scores, keys)
        both = dot_nn(d_scores, sorted_q[j])
        key_before[j] = both[:rows]
        key_own[j] = both[rows:]

    def query_gradients(place):
        j = place + base
        q = sorted_q[j].astype(F32)
        dk = key_own[j] + key_before[after(j)]
        scale = lax.rsqrt(jnp.mean(q * q, axis=-1, keepdims=True) + EPS)
        along = jnp.mean(q * dk, axis=-1, keepdims=True)
        pulled = (dk * scale - q * (scale * scale * scale * along)) / math.sqrt(depth)
        bucket_back(place, (d_query[j] + pulled).astype(BF16))


    def assemble(t):
        with jax.named_scope(f"wait_home{t}"):
            for step in near_first:
                homes[t][step].wait_recv()
        for head, part in enumerate(parts):
            total = home_in[t, head * split]
            for p in range(1, split):
                total = (total.astype(F32) + home_in[t, head * split + p].astype(F32)).astype(BF16)
            grads[t, :, part] = total

    def weight_gradient(t, half):
        with jax.named_scope(f"weight{half}"):
            for stream in range(streams):
                columns = slice(stream * piece, (stream + 1) * piece)
                grad = (dot_tn(normal[...], grads[t, :, columns]) * grad_scale).astype(BF16)
                weights[half, stream] = grad.reshape(devices, width // devices, piece)
            for stream in range(streams):
                for mask in forwarding_order(stages[0][half][stream]):
                    stages[0][half][stream][mask].start()

    outs = (d_qk_ref, d_v_ref)

    def run_sums(k, halves):
        waiting = []
        with jax.named_scope(f"sum{k}_{halves[0]}"):
            for half in halves:
                for masks in zip(*[forwarding_order(stages[k][half][s]) for s in range(streams)]):
                    for stream, mask in enumerate(masks):
                        rest = mask - (1 << k)
                        stages[k][half][stream][mask].wait_recv()
                        slot = first_slot[k] + (mask >> (k + 1))
                        came = sums_in[half, stream, slot].astype(F32)
                        if k == 0:
                            before = weights[half, stream, flipped(me, physical(stream, rest))]
                        else:
                            before = sums_run[half, stream, rest >> 1]
                        run = before.astype(F32) + came
                        if k == bits - 1:
                            outs[half][:, stream * piece : (stream + 1) * piece] = run
                            continue
                        sums_run[half, stream, rest >> 1] = run.astype(BF16)
                        waiting.append(stages[k + 1][half][stream].get(rest))
                        if len(waiting) > 1:
                            onward = waiting.pop(0)
                            if onward is not None:
                                onward.start()
            for onward in waiting:
                if onward is not None:
                    onward.start()

    with jax.named_scope("ds"):
        looped(queries, 16, score_gradients)
    assemble(0)
    weight_gradient(0, 1)
    with jax.named_scope("dq"):
        looped(held, 16, query_gradients)
    run_sums(0, (1,))
    send_home(1)
    d_normal = dot_nt(grads[0], v_ref[...])
    run_sums(1, (1,))
    assemble(1)
    weight_gradient(1, 0)
    with jax.named_scope("rows"):
        d_normal += dot_nt(grads[1], qk_ref[...])
        x = tokens_ref[...].astype(F32)
        scale = lax.rsqrt(jnp.mean(x * x, axis=-1, keepdims=True) + EPS)
        gain_total = jnp.sum(d_normal * (x * scale), axis=0, keepdims=True) * grad_scale
        share = width // devices
        gain_out[...] = jnp.zeros(gain_out.shape, F32)
        for device in range(devices):
            gain_out[device, 0:1, 0:share] = gain_total[:, device * share : (device + 1) * share]
        gain_back[me] = gain_out[me]
        for copy in gains:
            copy.start()
        t = d_normal * gain_ref[...]
        along = jnp.mean(x * t, axis=-1, keepdims=True)
        d_tokens_ref[...] = (t * scale - x * (scale * scale * scale * along)).astype(BF16)

    run_sums(0, (0,))
    run_sums(2, (1,))
    run_sums(1, (0,))
    for k in range(2, bits):
        run_sums(k, (0,))
        if k + 1 < bits:
            run_sums(k + 1, (1,))
    with jax.named_scope("sendwaits"):
        for copy in gains:
            copy.wait_recv()
        d_gain_ref[...] = jnp.sum(gain_back[:, 0, :], axis=0, keepdims=True)
        for stage in stages:
            for half in stage:
                for stream in half:
                    for copy in stream.values():
                        copy.wait_send()
        for group in [*slabs, *relays, shares[-1], *homes]:
            for copy in group.values():
                copy.wait_send()
        for copy in [*row_sums, *gains]:
            copy.wait_send()


def hand_over(share, d_tokens_in, d_gain_in, d_qk_in, d_v_in, d_tokens, d_gain, d_qk, d_v):
    d_tokens[...] = d_tokens_in[...]
    d_gain[...] = d_gain_in[:, :share]
    d_qk[...] = d_qk_in[...]
    d_v[...] = d_v_in[...]


def per_device(tokens, norm_gain, w_qk, w_v, cotangent, log_sums, bucket_order, token_position):
    devices = lax.axis_size("tok")
    tok_dev, width = tokens.shape
    rounds, seq_len = bucket_order.shape
    heads = log_sums.shape[1]
    units = rounds * heads
    assert tok_dev == BLOCK and devices % units == 0
    split = devices // units
    chips = devices // rounds
    depth = width // heads
    queries = seq_len // tok_dev // split
    held = queries if split == 1 else queries + 1
    capacity = 5 * tok_dev // (4 * devices)
    stride = -(-capacity // 8) * 8
    grad_scale = 1.0 / math.sqrt(seq_len)
    share = width // devices
    dma = pltpu.SemaphoreType.DMA

    def low(*shape):
        return pltpu.VMEM(shape, BF16)

    def full(*shape):
        return pltpu.VMEM(shape, F32)

    results = pl.pallas_call(
        functools.partial(core_kernel, heads, stride, split, grad_scale),
        out_shape=[
            jax.ShapeDtypeStruct((tok_dev, width), BF16),
            jax.ShapeDtypeStruct((1, 128), F32),
            jax.ShapeDtypeStruct((share, width), F32),
            jax.ShapeDtypeStruct((share, width), F32),
        ],
        in_specs=[pl.BlockSpec(memory_space=pl.ANY)] * 7,
        out_specs=whole(4),
        scratch_shapes=[
            full(1, width),
            pltpu.VMEM((rounds, seq_len), jnp.int32),
            full(rounds, heads, tok_dev),
            low(tok_dev, width),
            low(tok_dev, width),
            low(width, width),
            low(width, width),
            low(tok_dev, width),
            low(3, heads, tok_dev, depth),
            low(3, rounds, chips, tok_dev, depth),
            full(units, 1, tok_dev),
            full(devices, 1, tok_dev),
            low(devices, held, stride, tok_dev),
            low(held, devices * stride, tok_dev),
            low(devices, held, stride, depth),
            *[low(queries + 2, tok_dev, depth)] * 4,
            low(queries + 2, 2 * tok_dev, tok_dev),
            *[full(queries + 2, tok_dev, depth)] * 3,
            low(rounds - 1, chips, tok_dev, depth),
            low(2, rounds - 1, chips, tok_dev, depth),
            *[low(2, chips, tok_dev, depth)] * 2,
            low(2, tok_dev, width),
            *[full(devices, 8, 128)] * 2,
            low(2, 2, devices, share, width // 2),
            low(2, 2, devices - 1, share, width // 2),
            low(2, 2, devices // 2, share, width // 2),
            dma((7,)),
            dma((3, chips - 1, 2)),
            dma((3, rounds - 1, chips, 2)),
            dma((devices - 1, 2)),
            dma((2, rounds - 1, chips, 2)),
            dma((2, chips - 1, 2)),
            dma((devices - 1, 2)),
            dma((2, 2, devices - 1, 2)),
        ],
        compiler_params=pltpu.CompilerParams(
            vmem_limit_bytes=VMEM_LIMIT, collective_id=0, has_side_effects=True
        ),
        name="core",
    )(norm_gain.reshape(1, width), bucket_order, log_sums, tokens, cotangent, w_qk, w_v)
    d_tokens, d_gain, d_qk, d_v = pl.pallas_call(
        functools.partial(hand_over, share),
        out_shape=[
            jax.ShapeDtypeStruct((tok_dev, width), BF16),
            jax.ShapeDtypeStruct((1, share), F32),
            jax.ShapeDtypeStruct((share, width), F32),
            jax.ShapeDtypeStruct((share, width), F32),
        ],
        in_specs=whole(4),
        out_specs=whole(4),
        name="hand_over",
    )(*results)
    return (d_tokens, d_gain.reshape(share), d_qk, d_v)


def solution(mesh):
    in_specs = (
        P(("groups", "tok"), None),
        P(),
        P(),
        P(),
        P(("groups", "tok"), None),
        P(None, None, ("groups", "tok")),
        P(None, "groups"),
        P(None, ("groups", "tok")),
    )
    out_specs = (
        P(("groups", "tok"), None),
        P(("groups", "tok")),
        P(("groups", "tok"), None),
        P(("groups", "tok"), None),
    )
    return jax.shard_map(
        per_device, mesh=mesh, in_specs=in_specs, out_specs=out_specs, check_vma=False
    )
```

profile of v0, /device:TPU:0, one launch (start us, length us, event | category | flops | bytes accessed | tf_op | source)
XLA Modules:
  0.0 107.4 jit_solution(14895005005667364643)
XLA Ops:
  0.6 104.6 %core.1 = (bf16[256,1024]{1,0:T(8,128)(2,1)}, f32[1,128]{1,0:T(1,128)}, f32[64,1024]{1,0:T(8,128)}, f32[64,1024]{1,0:T(8,128)}) custom-call(f32[1,1024]{1,0:T(1,128)} %bitcast.2, s32[2,4096]{1,0:T(2,128)} %refs_1_.1, f32[2,8,256]{2,1,0:T(8,128)} %refs_2_.1, bf16[256,1024]{1,0:T(8,128)(2,1)} %refs_3_.1, bf16[256,1024]{1,0:T(8,128)(2,1)} %refs_4_.1, ...), custom_call_target="tpu_custom_call" | custom-call | tf_op jit(solution)/shard_map/core/pallas_call | solution.py:591
  105.2 2.2 %hand_over.1 = (bf16[256,1024]{1,0:T(8,128)(2,1)}, f32[1,64]{1,0:T(1,128)}, f32[64,1024]{1,0:T(8,128)}, f32[64,1024]{1,0:T(8,128)}) custom-call(bf16[256,1024]{1,0:T(8,128)(2,1)} %get-tuple-element.12.d_tokens_in, f32[1,128]{1,0:T(1,128)} %get-tuple-element.13.d_gain_in, f32[64,1024]{1,0:T(8,128)} %get-tuple-element.14.d_qk_in, ...), custom_call_target="tpu_custom_call" | custom-call | tf_op jit(solution)/shard_map/hand_over/pallas_call | solution.py:642
where the time goes:
time: 108 us; the launch traced here: 107 us
  Pallas kernels  107 us (99%)
    pallas_call x1, Pallas kernels, per_device(): pl.pallas_call(functools.partial(core_kernel, heads, stride, split, grad_...  105 us
    pallas_call x1, Pallas kernels, per_device(): pl.pallas_call(functools.partial(hand_over, share), out_shape=[jax.ShapeD...  2.19 us

commit v1 on v0

--- a/solution.py
+++ b/solution.py
@@ -91,12 +91,12 @@
     gain_hbm, order_hbm, sums_hbm, tokens_hbm, cot_hbm, qk_hbm, v_hbm = refs[:7]
     d_tokens_ref, d_gain_ref, d_qk_ref, d_v_ref = refs[7:11]
     (
-        gain_ref, order_ref, sums_ref, tokens_ref, cot_ref, qk_ref, v_ref,
+        gain_ref, order_ref, sums_ref, tokens_ref, qk_ref, v_ref,
         normal, slab_out, slab_in, sums_out, sums_in_rows, spread, pick, bucket,
-        sorted_q, sorted_k, sorted_g, sorted_v, probs, key_own, key_before, d_query,
+        sorted_q, sorted_k, sorted_g, sorted_v, probs, d_query,
         part_out, part_in, home_out, home_in, grads,
         gain_out, gain_back, weights, sums_in, sums_run,
-        load_sem, slab_sem, relay_sem, rows_sem, part_sem, home_sem, gain_sem, sums_sem,
+        cot_sem, load_sem, slab_sem, relay_sem, rows_sem, part_sem, home_sem, gain_sem, sums_sem,
     ) = refs[11:]
     devices = lax.axis_size("tok")
     me = lax.axis_index("tok")
@@ -127,28 +127,29 @@
     for step in range(1, devices):
         peer = lax.rem(me + step, devices)
         pl.semaphore_signal(barrier, inc=1, device_id={"tok": peer}, device_id_type=MESH)
+    cot_loads = [
+        pltpu.make_async_copy(cot_hbm.at[:, part], slab_out.at[0, head], cot_sem.at[head])
+        for head, part in enumerate(parts)
+    ]
     loads = {
         name: pltpu.make_async_copy(src, dst, load_sem.at[place])
         for place, (name, src, dst) in enumerate(
             [
+                ("sums", sums_hbm, sums_ref),
                 ("tokens", tokens_hbm, tokens_ref),
                 ("gain", gain_hbm, gain_ref),
                 ("qk", qk_hbm, qk_ref),
-                ("sums", sums_hbm, sums_ref),
-                ("cot", cot_hbm, cot_ref),
+                ("v", v_hbm, v_ref),
                 ("order", order_hbm, order_ref),
-                ("v", v_hbm, v_ref),
             ]
         )
     }
-    for load in loads.values():
+    loads["sums"].start()
+    for load in cot_loads:
         load.start()
 
     def chip_at(step):
-        return lax.rem(chip + step, chips)
-
-    def chip_behind(step):
-        return lax.rem(chip + chips - step, chips)
+        return flipped(chip, step)
 
     def lane_at(step):
         return lax.rem(lane + step, rounds)
@@ -171,8 +172,8 @@
     relays = [
         {
             (d, step): remote(
-                slab_in.at[t, lane, chip_behind(step)],
-                slab_in.at[t, lane, chip_behind(step)],
+                slab_in.at[t, lane, chip_at(step)],
+                slab_in.at[t, lane, chip_at(step)],
                 relay_sem.at[t, d - 1, step],
                 chip * rounds + lane_at(d),
             )
@@ -189,8 +190,8 @@
     shares = [
         {
             (d, step): remote(
-                part_out.at[d - 1, step],
-                part_in.at[t, d - 1, step],
+                part_out.at[d - 1, chip_at(step)],
+                part_in.at[t, d - 1, chip_at(step)],
                 part_sem.at[t, d - 1, step],
                 chip * rounds + lane_at(d),
             )
@@ -202,7 +203,7 @@
     homes = [
         {
             step: remote(
-                home_out.at[t, step],
+                home_out.at[t, chip_at(step)],
                 home_in.at[t, chip],
                 home_sem.at[t, step - 1],
                 chip_at(step) * rounds + lane,
@@ -218,9 +219,16 @@
 
     bits = devices.bit_length() - 1
     first_slot = [devices - (devices >> k) for k in range(bits)]
-    bit_orders = [list(range(bits)), [0, *range(2, bits), 1]]
+    top = lax.div(chip, chips // 2)
+    sections = 2
+    by_section = [list(range(bits)), [0, *range(2, bits - 1), 1, bits - 1]]
+    bit_orders = by_section * 2
     streams = len(bit_orders)
-    piece = width // streams
+    half_width = width // 2
+    piece = half_width // sections
+
+    def half_start(group):
+        return pl.multiple_of(half_width * (top + group - 2 * top * group), half_width)
 
     def physical(stream, mask):
         return sum(1 << bit_orders[stream][k] for k in range(bits) if mask >> k & 1)
@@ -231,9 +239,14 @@
             source = weights.at[half, stream, flipped(me, physical(stream, mask))]
         else:
             source = sums_run.at[half, stream, mask >> 1]
-        peer = flipped(me, 1 << bit_orders[stream][k])
-        return remote(
-            source, sums_in.at[half, stream, slot], sums_sem.at[half, stream, slot], peer
+        landing = stream if k < bits - 1 else (stream + sections) % streams
+        return pltpu.make_async_remote_copy(
+            src_ref=source,
+            dst_ref=sums_in.at[half, landing, slot],
+            send_sem=sums_sem.at[half, stream, slot, 0],
+            recv_sem=sums_sem.at[half, landing, slot, 1],
+            device_id={"tok": flipped(me, 1 << bit_orders[stream][k])},
+            device_id_type=MESH,
         )
 
     stages = [
@@ -246,8 +259,8 @@
         ]
         for k in range(bits)
     ]
-    far_first = sorted(range(1, chips), key=lambda step: -min(step, chips - step))
-    near_first = far_first[::-1]
+    far_first = sorted(range(1, chips), key=lambda step: (-step.bit_length(), step))
+    near_first = list(range(1, chips))
 
     def send_slabs(t):
         for step in far_first:
@@ -255,20 +268,14 @@
         slab_in[t, lane, chip] = slab_out[t, lax.div(chip, split)]
 
     with jax.named_scope("first"):
-        loads["tokens"].wait()
-        loads["gain"].wait()
-        normal[...] = normal_of(tokens_ref[...].astype(F32), gain_ref[...])
-        loads["qk"].wait()
-        query = dot_nn(normal[...], qk_ref[...]).astype(BF16)
-        for head, part in enumerate(parts):
-            slab_out[0, head] = query[:, part]
         loads["sums"].wait()
         for hashing in range(rounds):
             for head in range(heads):
                 sums_out[head * rounds + hashing] = sums_ref[hashing, head : head + 1, :]
-        loads["cot"].wait()
-        for head, part in enumerate(parts):
-            slab_out[1, head] = cot_ref[:, part]
+        for load in cot_loads:
+            load.wait()
+        for name in ("tokens", "gain", "qk", "v", "order"):
+            loads[name].start()
     with jax.named_scope("barrier"):
         pl.semaphore_wait(barrier, devices - 1)
     with jax.named_scope("sends"):
@@ -277,6 +284,13 @@
         send_slabs(0)
         own_unit = lax.div(chip, split) * rounds + lane
         sums_in_rows[me] = sums_out[own_unit]
+        loads["tokens"].wait()
+        loads["gain"].wait()
+        normal[...] = normal_of(tokens_ref[...].astype(F32), gain_ref[...])
+        loads["qk"].wait()
+        query = dot_nn(normal[...], qk_ref[...]).astype(BF16)
+        for head, part in enumerate(parts):
+            slab_out[1, head] = query[:, part]
         send_slabs(1)
         loads["v"].wait()
         value = dot_nn(normal[...], v_ref[...]).astype(BF16)
@@ -318,11 +332,11 @@
 
     def gather(t):
         with jax.named_scope(f"gather{t}"):
-            looped(chips, 8, lambda step: bucket_rows(t, chip_behind(step), lane))
+            looped(chips, 8, lambda place: bucket_rows(t, place, lane))
             for d in range(1, rounds):
                 for step in [0, *near_first]:
                     relays[t][d, step].wait_recv()
-                looped(chips, 8, lambda step: bucket_rows(t, chip_behind(step), lane_behind(d)))
+                looped(chips, 8, lambda place: bucket_rows(t, place, lane_behind(d)))
 
     def sorted_rows(place):
         data = bucket[:, place].reshape(slot_count, depth)
@@ -333,10 +347,17 @@
         sorted_q[place + base] = q
         sorted_k[place + base] = unit_of(q.astype(F32))
 
+    def sort_cotangents(place):
+        sorted_g[place + base] = sorted_rows(place)
+
     take_slabs(0)
     gather(0)
+    with jax.named_scope("sortg"):
+        looped(held, 16, sort_cotangents)
+    take_slabs(1)
+    gather(1)
     with jax.named_scope("sortq"):
-        looped(held, 4, sort_queries)
+        looped(held, 16, sort_queries)
     if split == 1:
         sorted_k[0] = sorted_k[queries]
     with jax.named_scope("rowsums"):
@@ -352,7 +373,7 @@
         probs[i + 1] = jnp.where(diagonal, 0.0, jnp.exp(scores)).astype(BF16)
 
     with jax.named_scope("probs"):
-        looped(queries, 4, probabilities)
+        looped(queries, 8, probabilities)
     if split > 1:
         probs[0] = jnp.zeros((2 * rows, rows), BF16)
         probs[queries + 1] = jnp.zeros((2 * rows, rows), BF16)
@@ -361,8 +382,8 @@
     def after(j):
         return lax.rem(j, queries) + 1 if split == 1 else j + 1
 
-    def bucket_back(place, grad):
-        placed = dot_nn(pick[place], grad).astype(BF16)
+    def bucket_back(place):
+        placed = dot_nn(pick[place], sorted_v[place + base]).astype(BF16)
         bucket[:, place] = placed.reshape(devices, stride, depth)
 
     def home_rows(source_chip, source_lane):
@@ -377,46 +398,38 @@
                     copy.wait_send()
             for d in range(1, rounds):
 
-                def share(step):
-                    part_out[d - 1, step] = home_rows(chip_at(step), lane_at(d)).astype(BF16)
+                def share(place):
+                    part_out[d - 1, place] = home_rows(place, lane_at(d)).astype(BF16)
 
                 looped(chips, 8, share)
                 for step in [*far_first, 0]:
                     shares[t][d, step].start()
 
-            def keep(step):
-                d_query[step] = home_rows(chip_at(step), lane)
+            def keep(place):
+                d_query[place] = home_rows(place, lane)
 
             looped(chips, 8, keep)
             for step in [*far_first, 0]:
                 for d in range(1, rounds):
                     shares[t][d, step].wait_recv()
-
-            for step in [*far_first, 0]:
-                total = d_query[step]
+            for place in range(chips):
+                total = d_query[place]
                 for d in range(1, rounds):
-                    total += part_in[t, d - 1, step].astype(F32)
-                home_out[t, step] = total.astype(BF16)
+                    total += part_in[t, d - 1, place].astype(F32)
+                home_out[t, place] = total.astype(BF16)
             for step in far_first:
                 homes[t][step].start()
-            home_in[t, chip] = home_out[t, 0]
-
-    take_slabs(1)
-    gather(1)
-
-    def sort_cotangents(place):
-        sorted_g[place + base] = sorted_rows(place)
+            home_in[t, chip] = home_out[t, chip]
 
     def value_gradients(place):
         j = place + base
         grad = dot_nn(probs[j, rows:, :], sorted_g[j])
         grad += dot_nn(probs[after(j), :rows, :], sorted_g[after(j)])
-        bucket_back(place, grad.astype(BF16))
-
-    with jax.named_scope("sortg"):
-        looped(held, 16, sort_cotangents)
+        sorted_v[j] = grad.astype(BF16)
+
     with jax.named_scope("dv"):
         looped(held, 16, value_gradients)
+        looped(held, 16, bucket_back)
     send_home(0)
     take_slabs(2)
     gather(2)
@@ -429,97 +442,121 @@
     if split == 1:
         sorted_v[0] = sorted_v[queries]
     else:
-        key_own[0] = jnp.zeros((rows, depth), F32)
         d_query[0] = jnp.zeros((rows, depth), F32)
-        key_before[queries + 1] = jnp.zeros((rows, depth), F32)
+        sorted_q[queries + 1] = jnp.zeros((rows, depth), BF16)
 
     def score_gradients(i):
         j = i + 1
         values = sorted_v[pl.ds(i, 2)].reshape(2 * rows, depth)
-        keys = sorted_k[pl.ds(i, 2)].reshape(2 * rows, depth)
         w = probs[j].astype(F32)
         d_probs = dot_nt(values, sorted_g[j])
         delta = jnp.sum(w * d_probs, axis=0, keepdims=True)
-        d_scores = (w * (d_probs - delta)).astype(BF16)
-        d_query[j] = dot_tn(d_scores, keys)
-        both = dot_nn(d_scores, sorted_q[j])
-        key_before[j] = both[:rows]
-        key_own[j] = both[rows:]
-
-    def query_gradients(place):
+        probs[j] = (w * (d_probs - delta)).astype(BF16)
+
+    def query_gradients(i):
+        keys = sorted_k[pl.ds(i, 2)].reshape(2 * rows, depth)
+        d_query[i + 1] = dot_tn(probs[i + 1], keys)
+
+    def key_gradients(place):
         j = place + base
         q = sorted_q[j].astype(F32)
-        dk = key_own[j] + key_before[after(j)]
+        dk = dot_nn(probs[j, rows:, :], sorted_q[j])
+        dk += dot_nn(probs[after(j), :rows, :], sorted_q[after(j)])
         scale = lax.rsqrt(jnp.mean(q * q, axis=-1, keepdims=True) + EPS)
         along = jnp.mean(q * dk, axis=-1, keepdims=True)
         pulled = (dk * scale - q * (scale * scale * scale * along)) / math.sqrt(depth)
-        bucket_back(place, (d_query[j] + pulled).astype(BF16))
-
-
-    def assemble(t):
-        with jax.named_scope(f"wait_home{t}"):
-            for step in near_first:
+        sorted_v[j] = (d_query[j] + pulled).astype(BF16)
+
+    def assemble(t, group):
+        steps = [m for m in near_first if m.bit_length() <= bits - 2]
+        if group == 1:
+            steps = [m for m in near_first if m.bit_length() > bits - 2]
+        with jax.named_scope(f"wait_home{t}_{group}"):
+            for step in steps:
                 homes[t][step].wait_recv()
-        for head, part in enumerate(parts):
-            total = home_in[t, head * split]
+        half_heads = heads // 2
+        start = half_heads * (top + group - 2 * top * group)
+        for place in range(half_heads):
+            total = home_in[t, (start + place) * split]
             for p in range(1, split):
-                total = (total.astype(F32) + home_in[t, head * split + p].astype(F32)).astype(BF16)
-            grads[t, :, part] = total
-
-    def weight_gradient(t, half):
-        with jax.named_scope(f"weight{half}"):
-            for stream in range(streams):
-                columns = slice(stream * piece, (stream + 1) * piece)
-                grad = (dot_tn(normal[...], grads[t, :, columns]) * grad_scale).astype(BF16)
-                weights[half, stream] = grad.reshape(devices, width // devices, piece)
-            for stream in range(streams):
+                other = home_in[t, (start + place) * split + p]
+                total = (total.astype(F32) + other.astype(F32)).astype(BF16)
+            grads[t, group, :, parts[place]] = total
+
+    def weight_gradient(t, half, group):
+        with jax.named_scope(f"weight{half}_{group}"):
+            mine = range(group * sections, (group + 1) * sections)
+            for section, stream in enumerate(mine):
+                columns = slice(section * piece, (section + 1) * piece)
+                grad = dot_tn(normal[...], grads[t, group, :, columns]) * grad_scale
+                weights[half, stream] = grad.astype(BF16).reshape(devices, share, piece)
+            for stream in mine:
                 for mask in forwarding_order(stages[0][half][stream]):
                     stages[0][half][stream][mask].start()
 
+    def row_gradient(t, group, weight_ref):
+        return dot_nt(grads[t, group], weight_ref[:, pl.ds(half_start(group), half_width)])
+
     outs = (d_qk_ref, d_v_ref)
 
-    def run_sums(k, halves):
+    def run_sums(half, k, group):
+        mine = range(group * sections, (group + 1) * sections)
         waiting = []
-        with jax.named_scope(f"sum{k}_{halves[0]}"):
-            for half in halves:
-                for masks in zip(*[forwarding_order(stages[k][half][s]) for s in range(streams)]):
-                    for stream, mask in enumerate(masks):
-                        rest = mask - (1 << k)
-                        stages[k][half][stream][mask].wait_recv()
-                        slot = first_slot[k] + (mask >> (k + 1))
-                        came = sums_in[half, stream, slot].astype(F32)
-                        if k == 0:
-                            before = weights[half, stream, flipped(me, physical(stream, rest))]
-                        else:
-                            before = sums_run[half, stream, rest >> 1]
-                        run = before.astype(F32) + came
-                        if k == bits - 1:
-                            outs[half][:, stream * piece : (stream + 1) * piece] = run
-                            continue
-                        sums_run[half, stream, rest >> 1] = run.astype(BF16)
-                        waiting.append(stages[k + 1][half][stream].get(rest))
-                        if len(waiting) > 1:
-                            onward = waiting.pop(0)
-                            if onward is not None:
-                                onward.start()
+        with jax.named_scope(f"sum{half}_{k}_{group}"):
+            for masks in zip(*[forwarding_order(stages[k][half][s]) for s in mine]):
+                for stream, mask in zip(mine, masks):
+                    rest = mask - (1 << k)
+                    sender = stream if k < bits - 1 else (stream + sections) % streams
+                    stages[k][half][sender][mask].wait_recv()
+                    slot = first_slot[k] + (mask >> (k + 1))
+                    came = sums_in[half, stream, slot].astype(F32)
+                    if k == 0:
+                        before = weights[half, stream, flipped(me, physical(stream, rest))]
+                    else:
+                        before = sums_run[half, stream, rest >> 1]
+                    run = before.astype(F32) + came
+                    if k == bits - 1:
+                        column = half_start(group) + (stream - mine[0]) * piece
+                        outs[half][:, pl.ds(pl.multiple_of(column, piece), piece)] = run
+                        continue
+                    sums_run[half, stream, rest >> 1] = run.astype(BF16)
+                    waiting.append(stages[k + 1][half][stream].get(rest))
+                    if len(waiting) > 1:
+                        onward = waiting.pop(0)
+                        if onward is not None:
+                            onward.start()
             for onward in waiting:
                 if onward is not None:
                     onward.start()
 
+    share = width // devices
     with jax.named_scope("ds"):
         looped(queries, 16, score_gradients)
-    assemble(0)
-    weight_gradient(0, 1)
     with jax.named_scope("dq"):
-        looped(held, 16, query_gradients)
-    run_sums(0, (1,))
+        looped(queries, 16, query_gradients)
+    with jax.named_scope("dk"):
+        looped(held, 16, key_gradients)
+    with jax.named_scope("back"):
+        looped(held, 16, bucket_back)
     send_home(1)
-    d_normal = dot_nt(grads[0], v_ref[...])
-    run_sums(1, (1,))
-    assemble(1)
-    weight_gradient(1, 0)
+    assemble(0, 0)
+    weight_gradient(0, 1, 0)
+    assemble(0, 1)
+    weight_gradient(0, 1, 1)
+    run_sums(1, 0, 0)
+    run_sums(1, 0, 1)
+    d_normal = row_gradient(0, 0, v_ref) + row_gradient(0, 1, v_ref)
+    assemble(1, 0)
+    weight_gradient(1, 0, 0)
+    d_normal += row_gradient(1, 0, qk_ref)
+    run_sums(0, 0, 0)
+    run_sums(1, 1, 0)
+    run_sums(1, 1, 1)
+    assemble(1, 1)
+    weight_gradient(1, 0, 1)
+    d_normal += row_gradient(1, 1, qk_ref)
+    run_sums(0, 0, 1)
     with jax.named_scope("rows"):
-        d_normal += dot_nt(grads[1], qk_ref[...])
         x = tokens_ref[...].astype(F32)
         scale = lax.rsqrt(jnp.mean(x * x, axis=-1, keepdims=True) + EPS)
         gain_total = jnp.sum(d_normal * (x * scale), axis=0, keepdims=True) * grad_scale
@@ -534,13 +571,16 @@
         along = jnp.mean(x * t, axis=-1, keepdims=True)
         d_tokens_ref[...] = (t * scale - x * (scale * scale * scale * along)).astype(BF16)
 
-    run_sums(0, (0,))
-    run_sums(2, (1,))
-    run_sums(1, (0,))
+    run_sums(0, 1, 0)
+    run_sums(1, 2, 0)
+    run_sums(1, 2, 1)
+    run_sums(0, 1, 1)
     for k in range(2, bits):
-        run_sums(k, (0,))
-        if k + 1 < bits:
-            run_sums(k + 1, (1,))
+        run_sums(0, k, 0)
+        if k > 2:
+            run_sums(1, k, 0)
+            run_sums(1, k, 1)
+        run_sums(0, k, 1)
     with jax.named_scope("sendwaits"):
         for copy in gains:
             copy.wait_recv()
@@ -603,7 +643,6 @@
             pltpu.VMEM((rounds, seq_len), jnp.int32),
             full(rounds, heads, tok_dev),
             low(tok_dev, width),
-            low(tok_dev, width),
             low(width, width),
             low(width, width),
             low(tok_dev, width),
@@ -616,23 +655,24 @@
             low(devices, held, stride, depth),
             *[low(queries + 2, tok_dev, depth)] * 4,
             low(queries + 2, 2 * tok_dev, tok_dev),
-            *[full(queries + 2, tok_dev, depth)] * 3,
+            full(queries + 2, tok_dev, depth),
             low(rounds - 1, chips, tok_dev, depth),
             low(2, rounds - 1, chips, tok_dev, depth),
             *[low(2, chips, tok_dev, depth)] * 2,
-            low(2, tok_dev, width),
+            low(2, 2, tok_dev, width // 2),
             *[full(devices, 8, 128)] * 2,
-            low(2, 2, devices, share, width // 2),
-            low(2, 2, devices - 1, share, width // 2),
-            low(2, 2, devices // 2, share, width // 2),
-            dma((7,)),
+            low(2, 4, devices, share, width // 4),
+            low(2, 4, devices - 1, share, width // 4),
+            low(2, 4, devices // 2, share, width // 4),
+            dma((heads,)),
+            dma((6,)),
             dma((3, chips - 1, 2)),
             dma((3, rounds - 1, chips, 2)),
             dma((devices - 1, 2)),
             dma((2, rounds - 1, chips, 2)),
             dma((2, chips - 1, 2)),
             dma((devices - 1, 2)),
-            dma((2, 2, devices - 1, 2)),
+            dma((2, 4, devices - 1, 2)),
         ],
         compiler_params=pltpu.CompilerParams(
             vmem_limit_bytes=VMEM_LIMIT, collective_id=0, has_side_effects=True

time: 108 us -> 100 us (0.926)
  Pallas kernels: 107 us -> 98.6 us
    pallas_call x1, Pallas kernels: 105 us -> 96.4 us  [per_device(): pl.pallas_call(functools.partial(core_kernel, heads, stride, split, grad_...]
where the time goes in v1:
time: 100 us; the launch traced here: 99.2 us
  Pallas kernels  98.6 us (99%)
    pallas_call x1, Pallas kernels, per_device(): pl.pallas_call(functools.partial(core_kernel, heads, stride, split, grad_...  96.4 us
    pallas_call x1, Pallas kernels, per_device(): pl.pallas_call(functools.partial(hand_over, share), out_shape=[jax.ShapeD...  2.19 us

profile of v1, /device:TPU:0, one launch (start us, length us, event | category | flops | bytes accessed | tf_op | source)
XLA Modules:
  0.0 99.2 jit_solution(4884041245582745048)
XLA Ops:
  0.6 96.4 %core.1 = (bf16[256,1024]{1,0:T(8,128)(2,1)}, f32[1,128]{1,0:T(1,128)}, f32[64,1024]{1,0:T(8,128)}, f32[64,1024]{1,0:T(8,128)}) custom-call(f32[1,1024]{1,0:T(1,128)} %bitcast.2, s32[2,4096]{1,0:T(2,128)} %refs_1_.1, f32[2,8,256]{2,1,0:T(8,128)} %refs_2_.1, bf16[256,1024]{1,0:T(8,128)(2,1)} %refs_3_.1, bf16[256,1024]{1,0:T(8,128)(2,1)} %refs_4_.1, ...), custom_call_target="tpu_custom_call" | custom-call | tf_op jit(solution)/shard_map/core/pallas_call | solution.py:631
  97.0 2.2 %hand_over.1 = (bf16[256,1024]{1,0:T(8,128)(2,1)}, f32[1,64]{1,0:T(1,128)}, f32[64,1024]{1,0:T(8,128)}, f32[64,1024]{1,0:T(8,128)}) custom-call(bf16[256,1024]{1,0:T(8,128)(2,1)} %get-tuple-element.12.d_tokens_in, f32[1,128]{1,0:T(1,128)} %get-tuple-element.13.d_gain_in, f32[64,1024]{1,0:T(8,128)} %get-tuple-element.14.d_qk_in, ...), custom_call_target="tpu_custom_call" | custom-call | tf_op jit(solution)/shard_map/hand_over/pallas_call | solution.py:682

commit v2 on v1

--- a/solution.py
+++ b/solution.py
@@ -10,7 +10,7 @@
 
 BLOCK = 256
 EPS = 1e-06
-VMEM_LIMIT = 63 * 1024 * 1024
+VMEM_LIMIT = 62 * 1024 * 1024
 MESH = pl.DeviceIdType.MESH
 F32 = jnp.float32
 BF16 = jnp.bfloat16
@@ -89,15 +89,16 @@
 
 def core_kernel(heads, stride, split, grad_scale, *refs):
     gain_hbm, order_hbm, sums_hbm, tokens_hbm, cot_hbm, qk_hbm, v_hbm = refs[:7]
-    d_tokens_ref, d_gain_ref, d_qk_ref, d_v_ref = refs[7:11]
+    d_tokens_ref, d_gain_ref, d_weights_ref = refs[7:10]
     (
-        gain_ref, order_ref, sums_ref, tokens_ref, qk_ref, v_ref,
+        gain_ref, order_ref, sums_ref, tokens_ref, maps,
         normal, slab_out, slab_in, sums_out, sums_in_rows, spread, pick, bucket,
         sorted_q, sorted_k, sorted_g, sorted_v, probs, d_query,
-        part_out, part_in, home_out, home_in, grads,
+        part_out, part_in, home_out, home_in, grads, rows_kept, rows_out, rows_in, ends, ends_in,
         gain_out, gain_back, weights, sums_in, sums_run,
-        cot_sem, load_sem, slab_sem, relay_sem, rows_sem, part_sem, home_sem, gain_sem, sums_sem,
-    ) = refs[11:]
+        cot_sem, load_sem, slab_sem, relay_sem, rows_sem, part_sem, home_send_sem,
+        home_recv_sem, gain_sem, sums_sem, pair_sem,
+    ) = refs[10:]
     devices = lax.axis_size("tok")
     me = lax.axis_index("tok")
     rounds, seq_len = order_ref.shape
@@ -138,8 +139,8 @@
                 ("sums", sums_hbm, sums_ref),
                 ("tokens", tokens_hbm, tokens_ref),
                 ("gain", gain_hbm, gain_ref),
-                ("qk", qk_hbm, qk_ref),
-                ("v", v_hbm, v_ref),
+                ("qk", qk_hbm, maps.at[1]),
+                ("v", v_hbm, maps.at[0]),
                 ("order", order_hbm, order_ref),
             ]
         )
@@ -201,63 +202,91 @@
         for t in range(2)
     ]
     homes = [
-        {
-            step: remote(
-                home_out.at[t, chip_at(step)],
-                home_in.at[t, chip],
-                home_sem.at[t, step - 1],
-                chip_at(step) * rounds + lane,
+        [
+            pltpu.make_async_remote_copy(
+                src_ref=home_out.at[t, chip_at(step)],
+                dst_ref=home_in.at[lane, chip],
+                send_sem=home_send_sem.at[t, step],
+                recv_sem=home_recv_sem.at[step, lane],
+                device_id={"tok": chip_at(step) * rounds + t},
+                device_id_type=MESH,
             )
-            for step in range(1, chips)
-        }
+            for step in range(chips)
+        ]
         for t in range(2)
     ]
+    comings = [
+        [
+            pltpu.make_async_remote_copy(
+                src_ref=home_out.at[0, chip_at(step)],
+                dst_ref=home_in.at[l, chip_at(step)],
+                send_sem=home_send_sem.at[0, step],
+                recv_sem=home_recv_sem.at[step, l],
+                device_id={"tok": chip * rounds + 1 - lane},
+                device_id_type=MESH,
+            )
+            for l in range(rounds)
+        ]
+        for step in range(chips)
+    ]
+    other = 1 - lane
+    sibling = chip * rounds + other
+    normal_copy = remote(normal.at[lane], normal.at[lane], pair_sem.at[0], sibling)
+    rows_copy = remote(rows_out, rows_in, pair_sem.at[1], sibling)
     gains = []
     for step in range(1, devices):
         peer = lax.rem(me + step, devices)
         gains.append(remote(gain_out.at[peer], gain_back.at[me], gain_sem.at[step - 1], peer))
 
-    bits = devices.bit_length() - 1
-    first_slot = [devices - (devices >> k) for k in range(bits)]
+    bits = chips.bit_length() - 1
+    first_slot = [chips - (chips >> k) for k in range(bits)]
     top = lax.div(chip, chips // 2)
-    sections = 2
-    by_section = [list(range(bits)), [0, *range(2, bits - 1), 1, bits - 1]]
-    bit_orders = by_section * 2
-    streams = len(bit_orders)
     half_width = width // 2
-    piece = half_width // sections
+    y_first, y_late = list(range(bits)), [*range(1, bits - 1), 0, bits - 1]
+    late_start = 3 * half_width // 4
+    sections = [(y_first, slice(0, late_start)), (y_late, slice(late_start, half_width))]
 
     def half_start(group):
         return pl.multiple_of(half_width * (top + group - 2 * top * group), half_width)
 
-    def physical(stream, mask):
-        return sum(1 << bit_orders[stream][k] for k in range(bits) if mask >> k & 1)
-
-    def sums_copy(half, stream, k, mask):
+    def physical(bit_order, mask):
+        return sum(1 << bit_order[k] for k in range(bits) if mask >> k & 1)
+
+    def sums_copy(group, place, k, mask):
+        bit_order, columns = sections[place]
         slot = first_slot[k] + (mask >> (k + 1))
         if k == 0:
-            source = weights.at[half, stream, flipped(me, physical(stream, mask))]
+            source = weights.at[group, flipped(chip, physical(bit_order, mask)), :, columns]
         else:
-            source = sums_run.at[half, stream, mask >> 1]
-        landing = stream if k < bits - 1 else (stream + sections) % streams
+            source = sums_run.at[group, mask >> 1, :, columns]
+        landing = group if k < bits - 1 else 1 - group
         return pltpu.make_async_remote_copy(
             src_ref=source,
-            dst_ref=sums_in.at[half, landing, slot],
-            send_sem=sums_sem.at[half, stream, slot, 0],
-            recv_sem=sums_sem.at[half, landing, slot, 1],
-            device_id={"tok": flipped(me, 1 << bit_orders[stream][k])},
+            dst_ref=sums_in.at[landing, slot, :, columns],
+            send_sem=sums_sem.at[group, place, slot, 0],
+            recv_sem=sums_sem.at[landing, place, slot, 1],
+            device_id={"tok": flipped(chip, 1 << bit_order[k]) * rounds + lane},
             device_id_type=MESH,
         )
 
     stages = [
         [
             [
-                {m: sums_copy(half, stream, k, m) for m in range(1 << k, devices, 2 << k)}
-                for stream in range(streams)
+                {m: sums_copy(group, p, k, m) for m in range(1 << k, chips, 2 << k)}
+                for p in range(len(sections))
             ]
-            for half in range(2)
+            for group in range(2)
         ]
         for k in range(bits)
+    ]
+    end_copies = [
+        remote(
+            ends.at[other, :, pl.ds(half_start(group), half_width)],
+            ends_in.at[:, pl.ds(half_start(group), half_width)],
+            pair_sem.at[2 + group],
+            sibling,
+        )
+        for group in range(2)
     ]
     far_first = sorted(range(1, chips), key=lambda step: (-step.bit_length(), step))
     near_first = list(range(1, chips))
@@ -286,17 +315,19 @@
         sums_in_rows[me] = sums_out[own_unit]
         loads["tokens"].wait()
         loads["gain"].wait()
-        normal[...] = normal_of(tokens_ref[...].astype(F32), gain_ref[...])
+        rows_now = normal_of(tokens_ref[...].astype(F32), gain_ref[...])
+        normal[lane] = rows_now
         loads["qk"].wait()
-        query = dot_nn(normal[...], qk_ref[...]).astype(BF16)
+        query = dot_nn(rows_now, maps[1]).astype(BF16)
         for head, part in enumerate(parts):
             slab_out[1, head] = query[:, part]
         send_slabs(1)
         loads["v"].wait()
-        value = dot_nn(normal[...], v_ref[...]).astype(BF16)
+        value = dot_nn(normal[lane], maps[0]).astype(BF16)
         for head, part in enumerate(parts):
             slab_out[2, head] = value[:, part]
         send_slabs(2)
+        normal_copy.start()
         for t in range(3):
             for d in range(1, rounds):
                 relays[t][d, 0].start()
@@ -409,6 +440,8 @@
                 d_query[place] = home_rows(place, lane)
 
             looped(chips, 8, keep)
+            if t == 0:
+                take_slabs(2)
             for step in [*far_first, 0]:
                 for d in range(1, rounds):
                     shares[t][d, step].wait_recv()
@@ -417,9 +450,17 @@
                 for d in range(1, rounds):
                     total += part_in[t, d - 1, place].astype(F32)
                 home_out[t, place] = total.astype(BF16)
-            for step in far_first:
+            for step in near_first:
                 homes[t][step].start()
-            home_in[t, chip] = home_out[t, chip]
+
+            @pl.when(lane == t)
+            def _():
+                home_in[lane, chip] = home_out[t, chip]
+
+            @pl.when(lane != t)
+            def _():
+                homes[t][0].start()
+
 
     def value_gradients(place):
         j = place + base
@@ -431,7 +472,6 @@
         looped(held, 16, value_gradients)
         looped(held, 16, bucket_back)
     send_home(0)
-    take_slabs(2)
     gather(2)
 
     def sort_values(place):
@@ -467,60 +507,75 @@
         pulled = (dk * scale - q * (scale * scale * scale * along)) / math.sqrt(depth)
         sorted_v[j] = (d_query[j] + pulled).astype(BF16)
 
-    def assemble(t, group):
-        steps = [m for m in near_first if m.bit_length() <= bits - 2]
-        if group == 1:
-            steps = [m for m in near_first if m.bit_length() > bits - 2]
-        with jax.named_scope(f"wait_home{t}_{group}"):
+    def assemble(group):
+        steps = [m for m in range(chips) if (m.bit_length() == bits) == (group == 1)]
+        with jax.named_scope(f"wait_home{group}"):
             for step in steps:
-                homes[t][step].wait_recv()
+                if step > 0:
+                    for coming in comings[step]:
+                        coming.wait_recv()
+                else:
+                    pltpu.make_async_remote_copy(
+                        src_ref=home_out.at[0, chip],
+                        dst_ref=home_in.at[other, chip],
+                        send_sem=home_send_sem.at[0, 0],
+                        recv_sem=home_recv_sem.at[0, other],
+                        device_id={"tok": sibling},
+                        device_id_type=MESH,
+                    ).wait_recv()
         half_heads = heads // 2
         start = half_heads * (top + group - 2 * top * group)
-        for place in range(half_heads):
-            total = home_in[t, (start + place) * split]
-            for p in range(1, split):
-                other = home_in[t, (start + place) * split + p]
-                total = (total.astype(F32) + other.astype(F32)).astype(BF16)
-            grads[t, group, :, parts[place]] = total
-
-    def weight_gradient(t, half, group):
-        with jax.named_scope(f"weight{half}_{group}"):
-            mine = range(group * sections, (group + 1) * sections)
-            for section, stream in enumerate(mine):
-                columns = slice(section * piece, (section + 1) * piece)
-                grad = dot_tn(normal[...], grads[t, group, :, columns]) * grad_scale
-                weights[half, stream] = grad.astype(BF16).reshape(devices, share, piece)
-            for stream in mine:
-                for mask in forwarding_order(stages[0][half][stream]):
-                    stages[0][half][stream][mask].start()
-
-    def row_gradient(t, group, weight_ref):
-        return dot_nt(grads[t, group], weight_ref[:, pl.ds(half_start(group), half_width)])
-
-    outs = (d_qk_ref, d_v_ref)
-
-    def run_sums(half, k, group):
-        mine = range(group * sections, (group + 1) * sections)
+        for l in range(rounds):
+            for place in range(half_heads):
+                total = home_in[l, (start + place) * split]
+                for p in range(1, split):
+                    more = home_in[l, (start + place) * split + p]
+                    total = (total.astype(F32) + more.astype(F32)).astype(BF16)
+                grads[group, l * rows : (l + 1) * rows, parts[place]] = total
+
+    def weight_gradient(group):
+        with jax.named_scope(f"weight{group}"):
+            normals = normal[...].reshape(rounds * rows, width)
+            grad = dot_tn(normals, grads[group]) * grad_scale
+            weights[group] = grad.astype(BF16).reshape(chips, width // chips, half_width)
+            for copies in stages[0][group]:
+                for mask in forwarding_order(copies):
+                    copies[mask].start()
+
+    def row_gradients(group):
+        with jax.named_scope(f"rowgrad{group}"):
+            columns = pl.ds(half_start(group), half_width)
+            for l in range(rounds):
+                part = dot_nt(grads[group, l * rows : (l + 1) * rows], maps[lane, :, columns])
+                if group == 0:
+                    rows_kept[l] = part
+                else:
+                    rows_kept[l] += part
+
+    def run_sums(k, group):
         waiting = []
-        with jax.named_scope(f"sum{half}_{k}_{group}"):
-            for masks in zip(*[forwarding_order(stages[k][half][s]) for s in mine]):
-                for stream, mask in zip(mine, masks):
+        with jax.named_scope(f"sum{k}_{group}"):
+            for mask in forwarding_order(stages[k][group][0]):
+                for place, (bit_order, columns) in enumerate(sections):
                     rest = mask - (1 << k)
-                    sender = stream if k < bits - 1 else (stream + sections) % streams
-                    stages[k][half][sender][mask].wait_recv()
+                    sender = group if k < bits - 1 else 1 - group
+                    stages[k][sender][place][mask].wait_recv()
                     slot = first_slot[k] + (mask >> (k + 1))
-                    came = sums_in[half, stream, slot].astype(F32)
+                    came = sums_in[group, slot, :, columns].astype(F32)
                     if k == 0:
-                        before = weights[half, stream, flipped(me, physical(stream, rest))]
+                        row = flipped(chip, physical(bit_order, rest))
+                        before = weights[group, row, :, columns]
                     else:
-                        before = sums_run[half, stream, rest >> 1]
+                        before = sums_run[group, rest >> 1, :, columns]
                     run = before.astype(F32) + came
                     if k == bits - 1:
-                        column = half_start(group) + (stream - mine[0]) * piece
-                        outs[half][:, pl.ds(pl.multiple_of(column, piece), piece)] = run
+                        column = pl.multiple_of(half_start(group) + columns.start, 128)
+                        into = pl.ds(column, columns.stop - columns.start)
+                        for l in range(rounds):
+                            ends[l, :, into] = run[l * share : (l + 1) * share]
                         continue
-                    sums_run[half, stream, rest >> 1] = run.astype(BF16)
-                    waiting.append(stages[k + 1][half][stream].get(rest))
+                    sums_run[group, rest >> 1, :, columns] = run.astype(BF16)
+                    waiting.append(stages[k + 1][group][place].get(rest))
                     if len(waiting) > 1:
                         onward = waiting.pop(0)
                         if onward is not None:
@@ -528,6 +583,8 @@
             for onward in waiting:
                 if onward is not None:
                     onward.start()
+            if k == bits - 1:
+                end_copies[group].start()
 
     share = width // devices
     with jax.named_scope("ds"):
@@ -539,23 +596,21 @@
     with jax.named_scope("back"):
         looped(held, 16, bucket_back)
     send_home(1)
-    assemble(0, 0)
-    weight_gradient(0, 1, 0)
-    assemble(0, 1)
-    weight_gradient(0, 1, 1)
-    run_sums(1, 0, 0)
-    run_sums(1, 0, 1)
-    d_normal = row_gradient(0, 0, v_ref) + row_gradient(0, 1, v_ref)
-    assemble(1, 0)
-    weight_gradient(1, 0, 0)
-    d_normal += row_gradient(1, 0, qk_ref)
-    run_sums(0, 0, 0)
-    run_sums(1, 1, 0)
-    run_sums(1, 1, 1)
-    assemble(1, 1)
-    weight_gradient(1, 0, 1)
-    d_normal += row_gradient(1, 1, qk_ref)
-    run_sums(0, 0, 1)
+    normal_copy.wait_recv()
+    assemble(0)
+    weight_gradient(0)
+    row_gradients(0)
+    run_sums(0, 0)
+    assemble(1)
+    weight_gradient(1)
+    row_gradients(1)
+    rows_out[...] = rows_kept[other].astype(BF16)
+    rows_copy.start()
+    for k in range(1, bits - 1):
+        run_sums(k, 0)
+        run_sums(k - 1, 1)
+    rows_copy.wait_recv()
+    d_normal = rows_kept[lane] + rows_in[...].astype(F32)
     with jax.named_scope("rows"):
         x = tokens_ref[...].astype(F32)
         scale = lax.rsqrt(jnp.mean(x * x, axis=-1, keepdims=True) + EPS)
@@ -571,37 +626,50 @@
         along = jnp.mean(x * t, axis=-1, keepdims=True)
         d_tokens_ref[...] = (t * scale - x * (scale * scale * scale * along)).astype(BF16)
 
-    run_sums(0, 1, 0)
-    run_sums(1, 2, 0)
-    run_sums(1, 2, 1)
-    run_sums(0, 1, 1)
-    for k in range(2, bits):
-        run_sums(0, k, 0)
-        if k > 2:
-            run_sums(1, k, 0)
-            run_sums(1, k, 1)
-        run_sums(0, k, 1)
+    run_sums(bits - 2, 1)
+    run_sums(bits - 1, 0)
+    run_sums(bits - 1, 1)
+    with jax.named_scope("ends"):
+        d_weights_ref[lane] = ends[lane]
+        for copy in end_copies:
+            copy.wait_recv()
+        d_weights_ref[other] = ends_in[...]
     with jax.named_scope("sendwaits"):
         for copy in gains:
             copy.wait_recv()
         d_gain_ref[...] = jnp.sum(gain_back[:, 0, :], axis=0, keepdims=True)
         for stage in stages:
-            for half in stage:
-                for stream in half:
-                    for copy in stream.values():
-                        copy.wait_send()
-        for group in [*slabs, *relays, shares[-1], *homes]:
+            for copies in [*stage[0], *stage[1]]:
+                for copy in copies.values():
+                    copy.wait_send()
+        for group in [*slabs, *relays, shares[-1]]:
             for copy in group.values():
                 copy.wait_send()
-        for copy in [*row_sums, *gains]:
+        for t in range(2):
+            for step in range(1, chips):
+                homes[t][step].wait_send()
+        pltpu.make_async_remote_copy(
+            src_ref=home_out.at[0, chip],
+            dst_ref=home_in.at[lane, chip],
+            send_sem=home_send_sem.at[other, 0],
+            recv_sem=home_recv_sem.at[0, lane],
+            device_id={"tok": sibling},
+            device_id_type=MESH,
+        ).wait_send()
+        for copy in [*row_sums, *gains, normal_copy, rows_copy, *end_copies]:
             copy.wait_send()
 
 
-def hand_over(share, d_tokens_in, d_gain_in, d_qk_in, d_v_in, d_tokens, d_gain, d_qk, d_v):
-    d_tokens[...] = d_tokens_in[...]
+def hand_over(share, d_tokens_in, d_gain_in, d_weights_in, d_tokens, d_gain, d_qk, d_v, sems):
+    pairs = [
+        (d_tokens_in, d_tokens), (d_weights_in.at[1], d_qk), (d_weights_in.at[0], d_v)
+    ]
+    copies = [pltpu.make_async_copy(*pair, sems.at[i]) for i, pair in enumerate(pairs)]
+    for copy in copies:
+        copy.start()
     d_gain[...] = d_gain_in[:, :share]
-    d_qk[...] = d_qk_in[...]
-    d_v[...] = d_v_in[...]
+    for copy in copies:
+        copy.wait()
 
 
 def per_device(tokens, norm_gain, w_qk, w_v, cotangent, log_sums, bucket_order, token_position):
@@ -610,7 +678,7 @@
     rounds, seq_len = bucket_order.shape
     heads = log_sums.shape[1]
     units = rounds * heads
-    assert tok_dev == BLOCK and devices % units == 0
+    assert tok_dev == BLOCK and devices % units == 0 and rounds == 2
     split = devices // units
     chips = devices // rounds
     depth = width // heads
@@ -621,6 +689,7 @@
     grad_scale = 1.0 / math.sqrt(seq_len)
     share = width // devices
     dma = pltpu.SemaphoreType.DMA
+    hbm, vmem = pl.ANY, pltpu.VMEM
 
     def low(*shape):
         return pltpu.VMEM(shape, BF16)
@@ -631,21 +700,19 @@
     results = pl.pallas_call(
         functools.partial(core_kernel, heads, stride, split, grad_scale),
         out_shape=[
-            jax.ShapeDtypeStruct((tok_dev, width), BF16),
-            jax.ShapeDtypeStruct((1, 128), F32),
-            jax.ShapeDtypeStruct((share, width), F32),
-            jax.ShapeDtypeStruct((share, width), F32),
+            low(tok_dev, width),
+            full(1, 128),
+            full(2, share, width),
         ],
         in_specs=[pl.BlockSpec(memory_space=pl.ANY)] * 7,
-        out_specs=whole(4),
+        out_specs=whole(3),
         scratch_shapes=[
             full(1, width),
             pltpu.VMEM((rounds, seq_len), jnp.int32),
             full(rounds, heads, tok_dev),
             low(tok_dev, width),
-            low(width, width),
-            low(width, width),
-            low(tok_dev, width),
+            low(2, width, width),
+            low(rounds, tok_dev, width),
             low(3, heads, tok_dev, depth),
             low(3, rounds, chips, tok_dev, depth),
             full(units, 1, tok_dev),
@@ -659,20 +726,26 @@
             low(rounds - 1, chips, tok_dev, depth),
             low(2, rounds - 1, chips, tok_dev, depth),
             *[low(2, chips, tok_dev, depth)] * 2,
-            low(2, 2, tok_dev, width // 2),
+            low(2, rounds * tok_dev, width // 2),
+            full(rounds, tok_dev, width),
+            *[low(tok_dev, width)] * 2,
+            full(rounds, share, width),
+            full(share, width),
             *[full(devices, 8, 128)] * 2,
-            low(2, 4, devices, share, width // 4),
-            low(2, 4, devices - 1, share, width // 4),
-            low(2, 4, devices // 2, share, width // 4),
+            low(2, chips, width // chips, width // 2),
+            low(2, chips - 1, width // chips, width // 2),
+            low(2, chips // 2, width // chips, width // 2),
             dma((heads,)),
             dma((6,)),
             dma((3, chips - 1, 2)),
             dma((3, rounds - 1, chips, 2)),
             dma((devices - 1, 2)),
             dma((2, rounds - 1, chips, 2)),
-            dma((2, chips - 1, 2)),
+            dma((2, chips)),
+            dma((chips, rounds)),
             dma((devices - 1, 2)),
-            dma((2, 4, devices - 1, 2)),
+            dma((2, 2, chips - 1, 2)),
+            dma((4, 2)),
         ],
         compiler_params=pltpu.CompilerParams(
             vmem_limit_bytes=VMEM_LIMIT, collective_id=0, has_side_effects=True
@@ -687,10 +760,11 @@
             jax.ShapeDtypeStruct((share, width), F32),
             jax.ShapeDtypeStruct((share, width), F32),
         ],
-        in_specs=whole(4),
-        out_specs=whole(4),
+        in_specs=whole(3),
+        out_specs=[pl.BlockSpec(memory_space=space) for space in (hbm, vmem, hbm, hbm)],
+        scratch_shapes=[dma((3,))],
         name="hand_over",
-    )(*results)
+    )(*[pltpu.with_memory_space_constraint(result, vmem) for result in results])
     return (d_tokens, d_gain.reshape(share), d_qk, d_v)
 
 

time: 100 us -> 96.8 us (0.968)
  Pallas kernels: 98.6 us -> 95.8 us
    pallas_call x1, Pallas kernels: 96.4 us -> 94.3 us  [per_device(): pl.pallas_call(functools.partial(core_kernel, heads, stride, split, grad_...]
where the time goes in v2:
time: 96.8 us; the launch traced here: 96.6 us
  Pallas kernels  95.8 us (99%)
    pallas_call x1, Pallas kernels, per_device(): pl.pallas_call(functools.partial(core_kernel, heads, stride, split, grad_...  94.3 us

profile of v2, /device:TPU:0, one launch (start us, length us, event | category | flops | bytes accessed | tf_op | source)
XLA Modules:
  0.0 96.6 jit_solution(8466556919002320476)
XLA Ops:
  0.6 94.3 %core.1 = (bf16[256,1024]{1,0:T(8,128)(2,1)S(1)}, f32[1,128]{1,0:T(1,128)S(1)}, f32[2,64,1024]{2,1,0:T(8,128)S(1)}) custom-call(f32[1,1024]{1,0:T(1,128)} %bitcast.2, s32[2,4096]{1,0:T(2,128)} %refs_1_.1, f32[2,8,256]{2,1,0:T(8,128)} %refs_2_.1, bf16[256,1024]{1,0:T(8,128)(2,1)} %refs_3_.1, bf16[256,1024]{1,0:T(8,128)(2,1)} %refs_4_.1, ...), custom_call_target="tpu_custom_call" | custom-call | tf_op jit(solution)/shard_map/core/pallas_call | solution.py:700
  94.9 1.5 %hand_over.1 = (bf16[256,1024]{1,0:T(8,128)(2,1)}, f32[1,64]{1,0:T(1,128)}, f32[64,1024]{1,0:T(8,128)}, f32[64,1024]{1,0:T(8,128)}) custom-call(bf16[256,1024]{1,0:T(8,128)(2,1)S(1)} %get-tuple-element.11.d_tokens_in, f32[1,128]{1,0:T(1,128)S(1)} %get-tuple-element.12.d_gain_in, f32[2,64,1024]{2,1,0:T(8,128)S(1)} %get-tuple-element.13.d_weights_in), custom_call_target="tpu_custom_call" | custom-call | tf_op jit(solution)/shard_map/hand_over/pallas_call | solution.py:755

commit v3 on v2

--- a/solution.py
+++ b/solution.py
@@ -129,7 +129,7 @@
         peer = lax.rem(me + step, devices)
         pl.semaphore_signal(barrier, inc=1, device_id={"tok": peer}, device_id_type=MESH)
     cot_loads = [
-        pltpu.make_async_copy(cot_hbm.at[:, part], slab_out.at[0, head], cot_sem.at[head])
+        pltpu.make_async_copy(cot_hbm.at[:, part], slab_out.at[1, head], cot_sem.at[head])
         for head, part in enumerate(parts)
     ]
     loads = {
@@ -145,9 +145,8 @@
             ]
         )
     }
-    loads["sums"].start()
-    for load in cot_loads:
-        load.start()
+    for name in ("tokens", "gain", "qk", "sums"):
+        loads[name].start()
 
     def chip_at(step):
         return flipped(chip, step)
@@ -297,14 +296,22 @@
         slab_in[t, lane, chip] = slab_out[t, lax.div(chip, split)]
 
     with jax.named_scope("first"):
+        loads["tokens"].wait()
+        loads["gain"].wait()
+        rows_now = normal_of(tokens_ref[...].astype(F32), gain_ref[...])
+        normal[lane] = rows_now
+        loads["qk"].wait()
+        for load in cot_loads:
+            load.start()
+        for name in ("v", "order"):
+            loads[name].start()
+        query = dot_nn(rows_now, maps[1]).astype(BF16)
+        for head, part in enumerate(parts):
+            slab_out[0, head] = query[:, part]
         loads["sums"].wait()
         for hashing in range(rounds):
             for head in range(heads):
                 sums_out[head * rounds + hashing] = sums_ref[hashing, head : head + 1, :]
-        for load in cot_loads:
-            load.wait()
-        for name in ("tokens", "gain", "qk", "v", "order"):
-            loads[name].start()
     with jax.named_scope("barrier"):
         pl.semaphore_wait(barrier, devices - 1)
     with jax.named_scope("sends"):
@@ -313,14 +320,8 @@
         send_slabs(0)
         own_unit = lax.div(chip, split) * rounds + lane
         sums_in_rows[me] = sums_out[own_unit]
-        loads["tokens"].wait()
-        loads["gain"].wait()
-        rows_now = normal_of(tokens_ref[...].astype(F32), gain_ref[...])
-        normal[lane] = rows_now
-        loads["qk"].wait()
-        query = dot_nn(rows_now, maps[1]).astype(BF16)
-        for head, part in enumerate(parts):
-            slab_out[1, head] = query[:, part]
+        for load in cot_loads:
+            load.wait()
         send_slabs(1)
         loads["v"].wait()
         value = dot_nn(normal[lane], maps[0]).astype(BF16)
@@ -361,9 +362,10 @@
                 for d in range(1, rounds):
                     relays[t][d, step].start()
 
-    def gather(t):
+    def gather(t, own=True):
         with jax.named_scope(f"gather{t}"):
-            looped(chips, 8, lambda place: bucket_rows(t, place, lane))
+            if own:
+                looped(chips, 8, lambda place: bucket_rows(t, place, lane))
             for d in range(1, rounds):
                 for step in [0, *near_first]:
                     relays[t][d, step].wait_recv()
@@ -383,10 +385,6 @@
 
     take_slabs(0)
     gather(0)
-    with jax.named_scope("sortg"):
-        looped(held, 16, sort_cotangents)
-    take_slabs(1)
-    gather(1)
     with jax.named_scope("sortq"):
         looped(held, 16, sort_queries)
     if split == 1:
@@ -442,6 +440,7 @@
             looped(chips, 8, keep)
             if t == 0:
                 take_slabs(2)
+                looped(chips, 8, lambda place: bucket_rows(2, place, lane))
             for step in [*far_first, 0]:
                 for d in range(1, rounds):
                     shares[t][d, step].wait_recv()
@@ -468,11 +467,15 @@
         grad += dot_nn(probs[after(j), :rows, :], sorted_g[after(j)])
         sorted_v[j] = grad.astype(BF16)
 
+    take_slabs(1)
+    gather(1)
+    with jax.named_scope("sortg"):
+        looped(held, 16, sort_cotangents)
     with jax.named_scope("dv"):
         looped(held, 16, value_gradients)
         looped(held, 16, bucket_back)
     send_home(0)
-    gather(2)
+    gather(2, own=False)
 
     def sort_values(place):
         sorted_v[place + base] = sorted_rows(place)

time: 96.8 us -> 94.8 us (0.979)
  Pallas kernels: 95.8 us -> 93.9 us
    pallas_call x1, Pallas kernels: 94.3 us -> 92.4 us  [per_device(): pl.pallas_call(functools.partial(core_kernel, heads, stride, split, grad_...]
where the time goes in v3:
time: 94.8 us; the launch traced here: 94.7 us
  Pallas kernels  93.9 us (99%)
    pallas_call x1, Pallas kernels, per_device(): pl.pallas_call(functools.partial(core_kernel, heads, stride, split, grad_...  92.4 us

profile of v3, /device:TPU:0, one launch (start us, length us, event | category | flops | bytes accessed | tf_op | source)
XLA Modules:
  0.0 94.7 jit_solution(1943560656661460995)
XLA Ops:
  0.6 92.4 %core.1 = (bf16[256,1024]{1,0:T(8,128)(2,1)S(1)}, f32[1,128]{1,0:T(1,128)S(1)}, f32[2,64,1024]{2,1,0:T(8,128)S(1)}) custom-call(f32[1,1024]{1,0:T(1,128)} %bitcast.2, s32[2,4096]{1,0:T(2,128)} %refs_1_.1, f32[2,8,256]{2,1,0:T(8,128)} %refs_2_.1, bf16[256,1024]{1,0:T(8,128)(2,1)} %refs_3_.1, bf16[256,1024]{1,0:T(8,128)(2,1)} %refs_4_.1, ...), custom_call_target="tpu_custom_call" | custom-call | tf_op jit(solution)/shard_map/core/pallas_call | solution.py:703
  93.0 1.5 %hand_over.1 = (bf16[256,1024]{1,0:T(8,128)(2,1)}, f32[1,64]{1,0:T(1,128)}, f32[64,1024]{1,0:T(8,128)}, f32[64,1024]{1,0:T(8,128)}) custom-call(bf16[256,1024]{1,0:T(8,128)(2,1)S(1)} %get-tuple-element.11.d_tokens_in, f32[1,128]{1,0:T(1,128)S(1)} %get-tuple-element.12.d_gain_in, f32[2,64,1024]{2,1,0:T(8,128)S(1)} %get-tuple-element.13.d_weights_in), custom_call_target="tpu_custom_call" | custom-call | tf_op jit(solution)/shard_map/hand_over/pallas_call | solution.py:758

commit v4 on v3

--- a/solution.py
+++ b/solution.py
@@ -606,11 +606,12 @@
     run_sums(0, 0)
     assemble(1)
     weight_gradient(1)
+    for k in range(1, bits - 1):
+        run_sums(k, 0)
     row_gradients(1)
     rows_out[...] = rows_kept[other].astype(BF16)
     rows_copy.start()
     for k in range(1, bits - 1):
-        run_sums(k, 0)
         run_sums(k - 1, 1)
     rows_copy.wait_recv()
     d_normal = rows_kept[lane] + rows_in[...].astype(F32)

time: 94.8 us -> 94.8 us (level)
  no operation moved by 1% of the time
where the time goes in v4:
time: 94.8 us; the launch traced here: 94.7 us
  Pallas kernels  93.9 us (99%)
    pallas_call x1, Pallas kernels, per_device(): pl.pallas_call(functools.partial(core_kernel, heads, stride, split, grad_...  92.4 us

profile of v4, /device:TPU:0, one launch (start us, length us, event | category | flops | bytes accessed | tf_op | source)
XLA Modules:
  0.0 94.7 jit_solution(12519780760580907681)
XLA Ops:
  0.6 92.4 %core.1 = (bf16[256,1024]{1,0:T(8,128)(2,1)S(1)}, f32[1,128]{1,0:T(1,128)S(1)}, f32[2,64,1024]{2,1,0:T(8,128)S(1)}) custom-call(f32[1,1024]{1,0:T(1,128)} %bitcast.2, s32[2,4096]{1,0:T(2,128)} %refs_1_.1, f32[2,8,256]{2,1,0:T(8,128)} %refs_2_.1, bf16[256,1024]{1,0:T(8,128)(2,1)} %refs_3_.1, bf16[256,1024]{1,0:T(8,128)(2,1)} %refs_4_.1, ...), custom_call_target="tpu_custom_call" | custom-call | tf_op jit(solution)/shard_map/core/pallas_call | solution.py:704
  93.0 1.5 %hand_over.1 = (bf16[256,1024]{1,0:T(8,128)(2,1)}, f32[1,64]{1,0:T(1,128)}, f32[64,1024]{1,0:T(8,128)}, f32[64,1024]{1,0:T(8,128)}) custom-call(bf16[256,1024]{1,0:T(8,128)(2,1)S(1)} %get-tuple-element.11.d_tokens_in, f32[1,128]{1,0:T(1,128)S(1)} %get-tuple-element.12.d_gain_in, f32[2,64,1024]{2,1,0:T(8,128)S(1)} %get-tuple-element.13.d_weights_in), custom_call_target="tpu_custom_call" | custom-call | tf_op jit(solution)/shard_map/hand_over/pallas_call | solution.py:759
